TPU v7x, 32 devices: a whole 2x2x4 slice. The times are simulated.
32 devices in a mesh: groups: 2 (over y), patch: 4 (over z), head: 4 (over x, core).
Axes of the slice: x: 2, y: 2, z: 4, core: 2. Of those that a mesh axis runs over, the one named last changes fastest.
Arguments:
- queries: bfloat16 [1536, 1536], P(('groups', 'patch'), 'head'), parts along dimension 0, may hold values from -12.5 to 12.5
- fresh_keys: bfloat16 [1536, 1536], P(('groups', 'patch'), 'head'), parts along dimension 0, may hold values from -5 to 5
- fresh_values: bfloat16 [1536, 1536], P(('groups', 'patch'), 'head'), parts along dimension 0, may hold values from -6 to 6
- stale_keys: bfloat16 [1536, 1536], P(('groups', 'patch'), 'head'), parts along dimension 0, may hold values from -5 to 5
- stale_values: bfloat16 [1536, 1536], P(('groups', 'patch'), 'head'), parts along dimension 0, may hold values from -6 to 6
- out_weight: bfloat16 [1536, 5120], P('head', 'patch'), may hold values from -0.21875 to 0.21875
- gate_scale: float32 [10240], P(('groups', 'head')), parts along dimension 0, may hold values from 1 to 4
Outputs:
- branch_out: float32 [1536, 5120], P(('groups', 'patch'), 'head'), parts along dimension 0
There are 2 independent parts, one for each index of `groups`. A program takes and returns all parts, laid end to end along the dimension named above; an argument that names none is the same for every part. Nothing has to cross between parts.
All inputs are finite; a program needn't handle non-finite values.
Results may differ from a plain program's by a relative error of at most 0.006.
Values may be sent and summed in bfloat16 or wider, within the bound.
No kernel may reach another device: no remote copies, remote signals or barrier semaphores. Data moves between devices by JAX's collectives and lax.ppermute only.
A program may use at most 64 MiB of HBM per device.

v0:
```python
import jax
import jax.numpy as jnp
from jax import lax
from jax.sharding import PartitionSpec as P

HEAD_DIM = 128
neg_large = -1e30


def head_view(matrix):
    return matrix.reshape(matrix.shape[0], -1, HEAD_DIM)


def block_scores(query_heads, key_block):
    return jnp.einsum(
        "qhd,khd->hqk", query_heads, head_view(key_block), preferred_element_type=jnp.float32
    ) * HEAD_DIM ** (-0.5)


def absorb(running, scores, value_block):
    run_max, run_total, run_acc = running
    new_max = jnp.maximum(run_max, jnp.max(scores, axis=2))
    factor = jnp.exp(run_max - new_max)
    weights = jnp.exp(scores - new_max[:, :, None])
    new_total = run_total * factor + jnp.sum(weights, axis=2)
    mixture = jnp.einsum(
        "hqk,khd->qhd",
        weights.astype(jnp.bfloat16),
        head_view(value_block),
        preferred_element_type=jnp.float32,
    )
    new_acc = run_acc * jnp.transpose(factor)[:, :, None] + mixture
    return (new_max, new_total, new_acc)


def empty_state(row_count, head_count):
    return (
        jnp.full((head_count, row_count), neg_large, jnp.float32),
        jnp.zeros((head_count, row_count), jnp.float32),
        jnp.zeros((row_count, head_count, HEAD_DIM), jnp.float32),
    )


def on_device(queries, fresh_keys, fresh_values, stale_keys, stale_values, out_weight, gate_scale):
    query_heads = head_view(queries)
    row_count = query_heads.shape[0]
    head_count = query_heads.shape[1]
    own_index = lax.axis_index("patch")
    own_start = own_index * row_count
    local = absorb(
        empty_state(row_count, head_count), block_scores(query_heads, fresh_keys), fresh_values
    )
    key_piece = lax.all_gather(stale_keys, "patch", axis=0, tiled=True)
    value_piece = lax.all_gather(stale_values, "patch", axis=0, tiled=True)
    key_count = key_piece.shape[0]
    key_step = 1024 if key_count > 1024 and key_count % 1024 == 0 else key_count

    def visit(block_index, inner):
        offset = block_index * key_step
        key_block = lax.dynamic_slice_in_dim(key_piece, offset, key_step, 0)
        value_block = lax.dynamic_slice_in_dim(value_piece, offset, key_step, 0)
        scores = block_scores(query_heads, key_block)
        position = offset + lax.iota(jnp.int32, key_step)
        own_rows = (position >= own_start) & (position < own_start + row_count)
        scores = jnp.where(own_rows[None, None, :], neg_large, scores)
        return absorb(inner, scores, value_block)

    run_max, run_total, run_acc = lax.fori_loop(0, key_count // key_step, visit, local)
    attended = (
        (run_acc / jnp.transpose(run_total)[:, :, None]).astype(jnp.bfloat16).reshape(row_count, -1)
    )
    partial_out = jnp.dot(
        attended,
        lax.all_gather(out_weight, "patch", axis=1, tiled=True),
        preferred_element_type=jnp.float32,
    )
    summed = lax.psum_scatter(partial_out, "head", scatter_dimension=1, tiled=True)
    return gate_scale[None, :] * summed


def solution(mesh):
    return jax.shard_map(
        on_device,
        mesh=mesh,
        in_specs=(
            P(("groups", "patch"), "head"),
            P(("groups", "patch"), "head"),
            P(("groups", "patch"), "head"),
            P(("groups", "patch"), "head"),
            P(("groups", "patch"), "head"),
            P("head", "patch"),
            P(("groups", "head")),
        ),
        out_specs=P(("groups", "patch"), "head"),
        check_vma=False,
    )
```

profile of v0, /device:TPU:0, one launch (start us, length us, event | category | flops | bytes accessed | tf_op | source)
XLA Modules:
  0.0 154.9 jit_solution(16892380855673942393)
XLA Ops:
  6.5 0.0 copy-start
  6.5 0.0 all-gather.2.cloned.1.call-start
  6.5 0.7 all-gather.2.cloned.1.call-update
  7.3 0.0 reduce-scatter.2.cloned.1.call-start
  7.3 0.0 copy-start.1
  7.3 20.8 %all_gather.9 = bf16[768,384]{1,0:T(8,128)(2,1)S(1)} all-gather(bf16[192,384]{1,0:T(8,128)(2,1)} %param.10), channel_id=1, replica_groups=mesh['groups'=2,'patch'=4,'head'=4] {'patch'}, dimensions={0}, use_global_device_ids=true | all-gather | bytes 737280 | tf_op jit(solution)/shard_map/all_gather | solution.py:53
  28.1 0.3 copy.27
  28.3 0.0 copy-done.2
  28.4 24.2 %all_gather.10 = bf16[768,384]{1,0:T(8,128)(2,1)S(1)} all-gather(bf16[192,384]{1,0:T(8,128)(2,1)S(1)} %copy-done.2), channel_id=1, replica_groups=mesh['groups'=2,'patch'=4,'head'=4] {'patch'}, dimensions={0}, use_global_device_ids=true | all-gather | bytes 737280 | tf_op jit(solution)/shard_map/all_gather | solution.py:54
  52.6 0.3 copy.30
  52.9 0.0 copy-done
  52.9 0.3 fusion.39
  53.2 0.5 fusion
  53.7 0.1 fusion.14
  53.8 0.5 fusion.1
  54.4 0.6 convolution_bitcast_fusion.1
  54.9 0.3 copy-done.4
  55.2 0.5 fusion.8
  55.7 43.2 %all-gather.2.cloned.1.call-done = bf16[384,5120]{1,0:T(8,128)(2,1)} async-done(((bf16[384,1280]{1,0:T(8,128)(2,1)}), bf16[384,5120]{1,0:T(8,128)(2,1)}) %all-gather.2.cloned.1.call-update) | async-done | bytes 3932176 | tf_op jit(solution)/shard_map/all_gather | solution.py:74
  98.9 5.2 %fusion.18 = f32[192,5120]{1,0:T(8,128)} fusion(bf16[384,5120]{1,0:T(8,128)(2,1)} %all-gather.2.cloned.1.call-done, bf16[3,24,8,128]{3,2,1,0:T(8,128)(2,1)S(1)} %fusion.8), kind=kOutput, calls=%fused_computation.23 | convolution fusion | flops 754974720 | bytes 8011776 | tf_op jit(solution)/shard_map/dot_general | solution.py:72
  104.1 0.0 reduce-scatter.2.cloned.1.call-update
  104.1 41.7 %reduce-scatter.2.cloned.1.call-done = f32[192,1280]{1,0:T(8,128)} async-done(((f32[192,5120]{1,0:T(8,128)}), f32[192,1280]{1,0:T(8,128)}) %reduce-scatter.2.cloned.1.call-update) | async-done | bytes 983056 | tf_op jit(solution)/shard_map/reduce_scatter | solution.py:77
  145.8 0.0 copy-done.3
  145.8 2.2 %broadcast_multiply_fusion = f32[192,1280]{1,0:T(8,128)} fusion(f32[192,1280]{1,0:T(8,128)} %reduce-scatter.2.cloned.1.call-done, f32[1280]{0:T(1024)S(1)} %copy-done.3), kind=kLoop, calls=%fused_computation.21 | loop fusion | flops 245760 | bytes 1971200 | tf_op jit(solution)/shard_map/mul | solution.py:78
  (7 shorter events, 0.0 us)
Async XLA Ops:
  6.5 46.3 %copy-start = (bf16[192,384]{1,0:T(8,128)(2,1)S(1)}, bf16[192,384]{1,0:T(8,128)(2,1)}, u32[]{:S(2)}) copy-start(bf16[192,384]{1,0:T(8,128)(2,1)} %param.7) | copy-start | bytes 442372
  6.5 21.8 %copy-start.2 = (bf16[192,384]{1,0:T(8,128)(2,1)S(1)}, bf16[192,384]{1,0:T(8,128)(2,1)}, u32[]{:S(2)}) copy-start(bf16[192,384]{1,0:T(8,128)(2,1)} %param.11) | copy-start | bytes 442372
  6.5 92.4 %all-gather.2.cloned.1.call-start = ((), (), s32[]{:S(2)}) async-start(), calls=%async_computation.1 | async-start | bytes 4915200 | tf_op jit(solution)/shard_map/all_gather | solution.py:74
  7.3 138.6 %reduce-scatter.2.cloned.1.call-start = ((), (), s32[]{:S(2)}) async-start(), calls=%async_computation.2 | async-start | bytes 4915200 | tf_op jit(solution)/shard_map/reduce_scatter | solution.py:77
  7.3 45.6 %copy-start.1 = (bf16[192,384]{1,0:T(8,128)(2,1)S(1)}, bf16[192,384]{1,0:T(8,128)(2,1)}, u32[]{:S(2)}) copy-start(bf16[192,384]{1,0:T(8,128)(2,1)} %param.8) | copy-start | bytes 442372
  54.3 0.9 copy-start.4
  104.1 41.8 %copy-start.3 = (f32[1280]{0:T(1024)S(1)}, f32[1280]{0:T(1024)}, u32[]{:S(2)}) copy-start(f32[1280]{0:T(1024)} %param.13) | copy-start | bytes 15364
Sparse Core Ops, SparseCore 0:
  8.9 89.9 all-gather.1
  104.2 41.5 reduce-scatter.1
where the time goes:
time: 155 us
  waiting for transfers between devices  85.7 us (55%)
  blocking collectives  45 us (29%)
  between operations  13.5 us (9%)
  matrix products  6.96 us (4%)
  other arithmetic  2.89 us (2%)
    all_gather x1, waiting for transfers between devices, on_device(): lax.all_gather(out_weight, 'patch', axis=1, tiled=True)  43.2 us
    reduce_scatter x1, waiting for transfers between devices, on_device(): lax.psum_scatter(partial_out, 'head', scatter_dimension=1, tiled=True)  41.7 us
    all_gather x1, blocking collectives, on_device(): value_piece = lax.all_gather(stale_values, 'patch', axis=0, tiled=True)  24.2 us
    all_gather x1, blocking collectives, on_device(): key_piece = lax.all_gather(stale_keys, 'patch', axis=0, tiled=True)  20.8 us
    dot_general x1, matrix products, on_device(): jnp.dot(attended, lax.all_gather(out_weight, 'patch', axis=1, tiled=True)...  5.18 us
  transfers between devices with their start and end apart: 2, of which 2 were waited for; matrix products, arithmetic and copies ran while one was open for 2% of the time, Pallas kernels for 0%

commit v1 on v0

--- a/solution.py
+++ b/solution.py
@@ -5,6 +5,19 @@
 
 HEAD_DIM = 128
 neg_large = -1e30
+
+
+def ring_gather(x, axis, dim):
+    size, here, rows = (lax.axis_size(axis), lax.axis_index(axis), x.shape[dim])
+    right = [(i, (i + 1) % size) for i in range(size)]
+    out = jnp.zeros((*x.shape[:dim], size * rows, *x.shape[dim + 1 :]), x.dtype)
+    held = x
+    for step in range(size):
+        holder = (here - step) % size
+        out = lax.dynamic_update_slice_in_dim(out, held, holder * rows, axis=dim)
+        if step < size - 1:
+            held = lax.ppermute(held, axis, right)
+    return out
 
 
 def head_view(matrix):
@@ -51,7 +64,7 @@
         empty_state(row_count, head_count), block_scores(query_heads, fresh_keys), fresh_values
     )
     key_piece = lax.all_gather(stale_keys, "patch", axis=0, tiled=True)
-    value_piece = lax.all_gather(stale_values, "patch", axis=0, tiled=True)
+    value_piece = ring_gather(stale_values, "patch", 0)
     key_count = key_piece.shape[0]
     key_step = 1024 if key_count > 1024 and key_count % 1024 == 0 else key_count
 

time: 155 us -> 158 us (1.019)
  blocking collectives: 45 us -> 23 us
  local copies, waits for them, and re-layouts: 0.84 us -> 14.1 us
  waiting for transfers between devices: 85.7 us -> 92.4 us
  starting transfers between devices: 0.04 us -> 4.4 us
    all_gather x1 -> x0, blocking collectives: 24.2 us -> none  [on_device(): value_piece = lax.all_gather(stale_values, 'patch', axis=0, tiled=True)]
    ppermute x0 -> x3, waiting for transfers between devices: none -> 20.7 us  [ring_gather(): held = lax.ppermute(held, axis, right)]
    all_gather x1, waiting for transfers between devices: 43.2 us -> 28.2 us  [on_device(): lax.all_gather(out_weight, 'patch', axis=1, tiled=True)]
    dynamic_update_slice x0 -> x4, local copies, waits for them, and re-layouts: none -> 12.7 us  [ring_gather(): out = lax.dynamic_update_slice_in_dim(out, held, holder * rows, axis=dim)]
    ppermute x0 -> x3, starting transfers between devices: none -> 4.36 us  [ring_gather(): held = lax.ppermute(held, axis, right)]
    all_gather x1, blocking collectives: 20.8 us -> 23 us  [on_device(): key_piece = lax.all_gather(stale_keys, 'patch', axis=0, tiled=True)]
  transfers between devices with their start and end apart: 2 -> 5, of which waited for: 2 -> 4; matrix products, arithmetic and copies ran while one was open for 2% -> 10% of each run, Pallas kernels for 0% -> 0%
where the time goes in v1:
time: 158 us; the launch traced here: 157 us
  waiting for transfers between devices  92.4 us (58%)
  blocking collectives  23 us (15%)
  local copies, waits for them, and re-layouts  14.1 us (9%)
  between operations  13.6 us (9%)
  matrix products  6.97 us (4%)
  starting transfers between devices  4.4 us (3%)
  other arithmetic  2.88 us (2%)
    reduce_scatter x1, waiting for transfers between devices, on_device(): lax.psum_scatter(partial_out, 'head', scatter_dimension=1, tiled=True)  42.8 us
    all_gather x1, waiting for transfers between devices, on_device(): lax.all_gather(out_weight, 'patch', axis=1, tiled=True)  28.2 us
    all_gather x1, blocking collectives, on_device(): key_piece = lax.all_gather(stale_keys, 'patch', axis=0, tiled=True)  23 us
    ppermute x3, waiting for transfers between devices, ring_gather(): held = lax.ppermute(held, axis, right)  20.7 us
    dynamic_update_slice x4, local copies, waits for them, and re-layouts, ring_gather(): out = lax.dynamic_update_slice_in_dim(out, held, holder * rows, axis=dim)  12.7 us
    dot_general x1, matrix products, on_device(): jnp.dot(attended, lax.all_gather(out_weight, 'patch', axis=1, tiled=True)...  5.21 us
    ppermute x3, starting transfers between devices, ring_gather(): held = lax.ppermute(held, axis, right)  4.36 us
  transfers between devices with their start and end apart: 5, of which 4 were waited for; matrix products, arithmetic and copies ran while one was open for 10% of the time, Pallas kernels for 0%

profile of v1, /device:TPU:0, one launch (start us, length us, event | category | flops | bytes accessed | tf_op | source)
XLA Modules:
  0.0 157.3 jit_solution(10245016405331228371)
XLA Ops:
  6.5 0.7 all-gather.2.cloned.1.call-update
  7.3 0.0 reduce-scatter.2.cloned.1.call-start
  7.3 1.0 copy.31
  8.4 3.1 %collective-permute-start = (bf16[192,384]{0,1:T(8,128)(2,1)S(1)}, bf16[192,384]{0,1:T(8,128)(2,1)}, u32[]{:S(2)}, u32[]{:S(2)}) collective-permute-start(bf16[192,384]{0,1:T(8,128)(2,1)S(1)} %copy.31), channel_id=1, source_target_pairs={{0,4},{4,8},{8,12},{12,0},{1,5},{5,9},{9,13},{13,1},{2,6},{6,10},{... | collective-permute-start | bytes 442376 | tf_op jit(solution)/shard_map/ppermute | solution.py:19
  11.5 23.0 %all_gather.6 = bf16[768,384]{1,0:T(8,128)(2,1)S(1)} all-gather(bf16[192,384]{1,0:T(8,128)(2,1)} %param.10), channel_id=1, replica_groups=mesh['groups'=2,'patch'=4,'head'=4] {'patch'}, dimensions={0}, use_global_device_ids=true | all-gather | bytes 737280 | tf_op jit(solution)/shard_map/all_gather | solution.py:66
  34.5 0.3 copy.28
  34.8 0.3 fusion.39
  35.0 0.5 fusion
  35.5 0.5 fusion.1
  36.2 2.6 %dynamic_update_slice.12 = bf16[768,384]{0,1:T(8,128)(2,1)S(1)} dynamic-update-slice(bf16[768,384]{0,1:T(8,128)(2,1)S(1)} %broadcast_in_dim.43, bf16[192,384]{0,1:T(8,128)(2,1)S(1)} %copy.31, s32[]{:T(128)S(6)} %select_n.41, s32[]{:T(128)} %constant.67.clone.1) | dynamic-update-slice | bytes 294916 | tf_op jit(solution)/shard_map/dynamic_update_slice | solution.py:17
  38.8 0.1 fusion.14
  38.9 0.8 collective-permute-start.1
  39.8 12.3 %collective-permute-done.1 = bf16[192,384]{0,1:T(8,128)(2,1)} collective-permute-done((bf16[192,384]{0,1:T(8,128)(2,1)}, bf16[192,384]{0,1:T(8,128)(2,1)}, u32[]{:S(2)}, u32[]{:S(2)}) %collective-permute-start.1) | collective-permute-done | bytes 147488 | tf_op jit(solution)/shard_map/ppermute | solution.py:19
  52.1 0.4 collective-permute-start.2
  52.5 0.4 fusion.4
  52.9 3.4 %dynamic_update_slice.13 = bf16[768,384]{0,1:T(8,128)(2,1)S(1)} dynamic-update-slice(bf16[768,384]{0,1:T(8,128)(2,1)S(1)} %dynamic_update_slice.12, bf16[192,384]{0,1:T(8,128)(2,1)} %collective-permute-done, s32[]{:T(128)S(6)} %select_n.43, s32[]{:T(128)} %constant.67.clone.1) | dynamic-update-slice | bytes 294916 | tf_op jit(solution)/shard_map/dynamic_update_slice | solution.py:17
  56.4 3.0 %dynamic_update_slice.14 = bf16[768,384]{0,1:T(8,128)(2,1)S(1)} dynamic-update-slice(bf16[768,384]{0,1:T(8,128)(2,1)S(1)} %dynamic_update_slice.13, bf16[192,384]{0,1:T(8,128)(2,1)} %collective-permute-done.1, s32[]{:T(128)S(6)} %select_n.45, s32[]{:T(128)} %constant.67.clone.1) | dynamic-update-slice | bytes 294916 | tf_op jit(solution)/shard_map/dynamic_update_slice | solution.py:17
  59.4 8.3 %collective-permute-done.2 = bf16[192,384]{0,1:T(8,128)(2,1)} collective-permute-done((bf16[192,384]{0,1:T(8,128)(2,1)}, bf16[192,384]{0,1:T(8,128)(2,1)}, u32[]{:S(2)}, u32[]{:S(2)}) %collective-permute-start.2) | collective-permute-done | bytes 147488 | tf_op jit(solution)/shard_map/ppermute | solution.py:19
  67.7 3.7 %dynamic_update_slice.15 = bf16[768,384]{0,1:T(8,128)(2,1)S(1)} dynamic-update-slice(bf16[768,384]{0,1:T(8,128)(2,1)S(1)} %dynamic_update_slice.14, bf16[192,384]{0,1:T(8,128)(2,1)} %collective-permute-done.2, s32[]{:T(128)S(6)} %select_n.47, s32[]{:T(128)} %constant.67.clone.1) | dynamic-update-slice | bytes 294916 | tf_op jit(solution)/shard_map/dynamic_update_slice | solution.py:17
  71.4 0.6 fusion.8
  72.0 28.2 %all-gather.2.cloned.1.call-done = bf16[384,5120]{1,0:T(8,128)(2,1)} async-done(((bf16[384,1280]{1,0:T(8,128)(2,1)}), bf16[384,5120]{1,0:T(8,128)(2,1)}) %all-gather.2.cloned.1.call-update) | async-done | bytes 3932176 | tf_op jit(solution)/shard_map/all_gather | solution.py:87
  100.2 5.2 %fusion.18 = f32[192,5120]{1,0:T(8,128)} fusion(bf16[384,5120]{1,0:T(8,128)(2,1)} %all-gather.2.cloned.1.call-done, bf16[3,24,8,128]{3,2,1,0:T(8,128)(2,1)S(1)} %fusion.8), kind=kOutput, calls=%fused_computation.23 | convolution fusion | flops 754974720 | bytes 8011776 | tf_op jit(solution)/shard_map/dot_general | solution.py:85
  105.4 42.8 %reduce-scatter.2.cloned.1.call-done = f32[192,1280]{1,0:T(8,128)} async-done(((f32[192,5120]{1,0:T(8,128)}), f32[192,1280]{1,0:T(8,128)}) %reduce-scatter.2.cloned.1.call-update) | async-done | bytes 983056 | tf_op jit(solution)/shard_map/reduce_scatter | solution.py:90
  148.2 2.2 %broadcast_multiply_fusion = f32[192,1280]{1,0:T(8,128)} fusion(f32[192,1280]{1,0:T(8,128)} %reduce-scatter.2.cloned.1.call-done, f32[1280]{0:T(1024)S(1)} %copy-done.3), kind=kLoop, calls=%fused_computation.21 | loop fusion | flops 245760 | bytes 1971200 | tf_op jit(solution)/shard_map/mul | solution.py:91
  (15 shorter events, 0.1 us)
Async XLA Ops:
  6.5 28.2 %copy-start = (bf16[192,384]{1,0:T(8,128)(2,1)S(1)}, bf16[192,384]{1,0:T(8,128)(2,1)}, u32[]{:S(2)}) copy-start(bf16[192,384]{1,0:T(8,128)(2,1)} %param.7) | copy-start | bytes 442372
  6.5 28.2 %copy-start.1 = (bf16[192,384]{1,0:T(8,128)(2,1)S(1)}, bf16[192,384]{1,0:T(8,128)(2,1)}, u32[]{:S(2)}) copy-start(bf16[192,384]{1,0:T(8,128)(2,1)} %param.8) | copy-start | bytes 442372
  6.5 93.7 %all-gather.2.cloned.1.call-start = ((), (), s32[]{:S(2)}) async-start(), calls=%async_computation.1 | async-start | bytes 4915200 | tf_op jit(solution)/shard_map/all_gather | solution.py:87
  7.3 141.0 %reduce-scatter.2.cloned.1.call-start = ((), (), s32[]{:S(2)}) async-start(), calls=%async_computation.2 | async-start | bytes 4915200 | tf_op jit(solution)/shard_map/reduce_scatter | solution.py:90
  8.4 30.6 %collective-permute-start = (bf16[192,384]{0,1:T(8,128)(2,1)S(1)}, bf16[192,384]{0,1:T(8,128)(2,1)}, u32[]{:S(2)}, u32[]{:S(2)}) collective-permute-start(bf16[192,384]{0,1:T(8,128)(2,1)S(1)} %copy.31), channel_id=1, source_target_pairs={{0,4},{4,8},{8,12},{12,0},{1,5},{5,9},{9,13},{13,1},{2,6},{6,10},{... | collective-permute-start | bytes 442376 | tf_op jit(solution)/shard_map/ppermute | solution.py:19
  35.5 17.0 %copy-start.2 = (bf16[192,384]{1,0:T(8,128)(2,1)S(1)}, bf16[192,384]{1,0:T(8,128)(2,1)}, u32[]{:S(2)}) copy-start(bf16[192,384]{1,0:T(8,128)(2,1)} %param.9) | copy-start | bytes 442372
  38.9 13.2 %collective-permute-start.1 = (bf16[192,384]{0,1:T(8,128)(2,1)}, bf16[192,384]{0,1:T(8,128)(2,1)}, u32[]{:S(2)}, u32[]{:S(2)}) collective-permute-start(bf16[192,384]{0,1:T(8,128)(2,1)} %collective-permute-done), channel_id=1, source_target_pairs={{0,4},{4,8},{8,12},{12,0},{1,5},{5,9},{9,13},{13,1},{2,6},{6,10},{... | collective-permute-start | bytes 442376 | tf_op jit(solution)/shard_map/ppermute | solution.py:19
  52.1 15.6 %collective-permute-start.2 = (bf16[192,384]{0,1:T(8,128)(2,1)}, bf16[192,384]{0,1:T(8,128)(2,1)}, u32[]{:S(2)}, u32[]{:S(2)}) collective-permute-start(bf16[192,384]{0,1:T(8,128)(2,1)} %collective-permute-done.1), channel_id=1, source_target_pairs={{0,4},{4,8},{8,12},{12,0},{1,5},{5,9},{9,13},{13,1},{2,6},{6,10},{... | collective-permute-start | bytes 442376 | tf_op jit(solution)/shard_map/ppermute | solution.py:19
  105.4 42.8 %copy-start.3 = (f32[1280]{0:T(1024)S(1)}, f32[1280]{0:T(1024)}, u32[]{:S(2)}) copy-start(f32[1280]{0:T(1024)} %param.13) | copy-start | bytes 15364
Sparse Core Ops, SparseCore 0:
  8.9 91.2 all-gather.1
  105.6 42.6 reduce-scatter.1
